TPU v7x, 1024 devices: a whole 4x4x32 slice. The times are simulated.
1024 devices in a mesh: section: 32 (over x, y, core), tensor: 8 (over z_lo), dp: 4 (over z_hi).
Axes of the slice: x: 4, y: 4, z: 32 (z_hi: 4, z_lo: 8; z = z_hi * 8 + z_lo), core: 2. Of those that a mesh axis runs over, the one named last changes fastest.
Arguments:
- fwd_input: bfloat16 [4, 32, 128, 8192], P('dp', 'section', None, 'tensor'), may hold values from -6 to 6
- fwd_positions: int32 [4, 32, 128], P('dp', 'section'), may hold values from 0 to 4095
- key_weight: bfloat16 [32, 8192, 4, 128], P('section', 'tensor'), may hold values from -0.0625 to 0.0625
- stash: bfloat16 [4, 32, 128, 8192], P('dp', 'section', None, 'tensor'), may hold values from -0.26367188 to 0.26367188
- partner: int32 [32], replicated, may hold values from 0 to 31, as said below
- key_grad: bfloat16 [4, 32, 128, 4, 128], P('dp', 'section'), may hold values from -6 to 6
- bwd_positions: int32 [4, 32, 128], P('dp', 'section'), may hold values from 0 to 4095
Outputs:
- key_out: bfloat16 [4, 32, 128, 4, 128], P('dp', 'section', 'tensor')
- grad_in: bfloat16 [4, 32, 128, 8192], P('dp', 'section', None, 'tensor')
- evicted: bfloat16 [4, 32, 128, 8192], P('dp', 'section', None, 'tensor')
- weight_grad: bfloat16 [32, 8192, 4, 128], P('section', ('tensor', 'dp'))
Inputs may be any that keep to these rules, and one draw needn't show every extreme that they name: partner[s] = s xor k for one k with 16 <= k < 32, the same k for all sections; it pairs every section of the first half with one of the second half.
All inputs are finite; a program needn't handle non-finite values.
Results may differ from a plain program's by a relative error of at most 0.015.
Values may be sent and summed in bfloat16 or wider, within the bound.
A program may use at most 32 MiB of HBM per device.

v0:
```python
import jax
import jax.numpy as jnp
from jax import lax
from jax.sharding import PartitionSpec as P

THETA = 500000.0


def from_behind(block, axis, distance):
    devices = range(lax.axis_size(axis))
    route = [((i - distance) % len(devices), i) for i in devices]
    return lax.ppermute(block, axis, route)


def swapped_2(value, axis, distance):
    return lax.ppermute(value, axis, [(i, i ^ 1 << distance) for i in range(lax.axis_size(axis))])


def rope_tables(positions, head_size):
    half = head_size // 2
    freqs = THETA ** (-(2.0 * jnp.arange(half, dtype=jnp.float32)) / head_size)
    angles = positions.astype(jnp.float32)[..., None] * freqs
    return (jnp.cos(angles), jnp.sin(angles))


def rotate(keys, cosine, sine, sign):
    half = keys.shape[-1] // 2
    first = keys[..., :half]
    second = keys[..., half:]
    return jnp.concatenate(
        [first * cosine - sign * second * sine, second * cosine + sign * first * sine], axis=-1
    )


def body(fwd_input, fwd_positions, key_weight, stash, partner, key_grad, bwd_positions):
    inputs = fwd_input[0, 0]
    weight = key_weight[0]
    width_local = weight.shape[0]
    head_count = weight.shape[1]
    head_size = weight.shape[2]
    flat_weight = weight.reshape(width_local, head_count * head_size)
    token_rows = inputs.shape[0]
    my_rows = token_rows // lax.axis_size("tensor")
    summed = lax.psum_scatter(
        jnp.dot(inputs, flat_weight, preferred_element_type=jnp.float32).astype(jnp.bfloat16),
        "tensor",
        scatter_dimension=0,
        tiled=True,
    ).astype(jnp.float32)
    summed = summed.reshape(my_rows, head_count, head_size)
    row_start = lax.axis_index("tensor") * my_rows
    my_positions = lax.dynamic_slice_in_dim(fwd_positions[0, 0], row_start, my_rows, 0)
    cosine, sine = rope_tables(my_positions, head_size)
    key_out = rotate(summed, cosine[:, None], sine[:, None], 1.0).astype(jnp.bfloat16)[None, None]
    grads = key_grad[0, 0].astype(jnp.float32)
    back_cos, back_sin = rope_tables(bwd_positions[0, 0], head_size)
    grad_pre = rotate(grads, back_cos[:, None], back_sin[:, None], -1.0).astype(jnp.bfloat16)
    grad_flat = grad_pre.reshape(token_rows, head_count * head_size)
    input_grad = jnp.einsum(
        "rn,dn->rd", grad_flat, flat_weight, preferred_element_type=jnp.float32
    ).astype(jnp.bfloat16)
    grad_in = from_behind(input_grad[None, None], "section", -1)
    mask_value = jnp.bitwise_xor(partner[0], 0)
    moving = jnp.stack([stash[0, 0], inputs])
    sections = lax.axis_size("section")
    levels = sections.bit_length() - 1
    for bit_number in range(levels):
        swapped = swapped_2(moving, "section", bit_number)
        moving = jnp.where(mask_value >> bit_number & 1 == 1, swapped, moving)
    held = moving[0]
    evicted = moving[1][None, None]
    grad_sum = lax.psum_scatter(
        jnp.einsum("rd,rn->dn", held, grad_flat, preferred_element_type=jnp.float32).astype(
            jnp.bfloat16
        ),
        "dp",
        scatter_dimension=0,
        tiled=True,
    ).astype(jnp.float32)
    weight_grad = grad_sum.astype(jnp.bfloat16).reshape(grad_sum.shape[0], head_count, head_size)[
        None
    ]
    return (key_out, grad_in, evicted, weight_grad)


def solution(mesh):
    placed = (
        P("dp", "section", None, "tensor"),
        P("dp", "section", None),
        P("section", "tensor", None, None),
        P("dp", "section", None, "tensor"),
        P(),
        P("dp", "section", None, None, None),
        P("dp", "section", None),
    )
    return jax.shard_map(
        body,
        mesh=mesh,
        in_specs=placed,
        out_specs=(
            P("dp", "section", "tensor", None, None),
            P("dp", "section", None, "tensor"),
            P("dp", "section", None, "tensor"),
            P("section", ("tensor", "dp"), None, None),
        ),
        check_vma=False,
    )
```

profile of v0, /device:TPU:10, one launch (start us, length us, event | category | flops | bytes accessed | tf_op | source)
XLA Modules:
  0.0 233.8 jit_solution(17653246110292259774)
XLA Ops:
  7.2 1.1 pad_maximum_fusion
  8.4 1.9 collective-permute-start.1
  10.3 1.8 collective-permute-done.1
  12.3 2.4 %collective-permute-start.2 = (bf16[2,128,1024]{2,1,0:T(8,128)(2,1)S(1)}, bf16[2,128,1024]{2,1,0:T(8,128)(2,1)S(1)}, u32[]{:S(2)}, u32[]{:S(2)}) collective-permute-start(bf16[2,128,1024]{2,1,0:T(8,128)(2,1)S(1)} %broadcast_select_fusion), channel_id=1, source_target_pairs={{0,64},{32,96},{64,0},{96,32},{128,192},{160,224},{192,128},{224,1... | collective-permute-start | bytes 1572872 | tf_op jit(solution)/shard_map/ppermute | solution.py:16
  14.7 13.5 %collective-permute-done.2 = bf16[2,128,1024]{2,1,0:T(8,128)(2,1)S(1)} collective-permute-done((bf16[2,128,1024]{2,1,0:T(8,128)(2,1)S(1)}, bf16[2,128,1024]{2,1,0:T(8,128)(2,1)S(1)}, u32[]{:S(2)}, u32[]{:S(2)}) %collective-permute-start.2) | collective-permute-done | bytes 524320 | tf_op jit(solution)/shard_map/ppermute | solution.py:16
  28.2 4.3 %collective-permute-start.3 = (bf16[2,128,1024]{2,1,0:T(8,128)(2,1)S(1)}, bf16[2,128,1024]{2,1,0:T(8,128)(2,1)S(1)}, u32[]{:S(2)}, u32[]{:S(2)}) collective-permute-start(bf16[2,128,1024]{2,1,0:T(8,128)(2,1)S(1)} %broadcast_select_fusion.1), channel_id=1, source_target_pairs={{0,128},{32,160},{64,192},{96,224},{128,0},{160,32},{192,64},{224,... | collective-permute-start | bytes 1572872 | tf_op jit(solution)/shard_map/ppermute | solution.py:16
  32.5 1.0 convolution_convert_fusion.2
  33.7 11.1 %collective-permute-done.3 = bf16[2,128,1024]{2,1,0:T(8,128)(2,1)S(1)} collective-permute-done((bf16[2,128,1024]{2,1,0:T(8,128)(2,1)S(1)}, bf16[2,128,1024]{2,1,0:T(8,128)(2,1)S(1)}, u32[]{:S(2)}, u32[]{:S(2)}) %collective-permute-start.3) | collective-permute-done | bytes 524320 | tf_op jit(solution)/shard_map/ppermute | solution.py:16
  44.9 14.1 %collective-permute-start.4 = (bf16[2,128,1024]{2,1,0:T(8,128)(2,1)S(1)}, bf16[2,128,1024]{2,1,0:T(8,128)(2,1)S(1)}, u32[]{:S(2)}, u32[]{:S(2)}) collective-permute-start(bf16[2,128,1024]{2,1,0:T(8,128)(2,1)S(1)} %broadcast_select_fusion.2), channel_id=1, source_target_pairs={{0,256},{32,288},{64,320},{96,352},{128,384},{160,416},{192,448},{... | collective-permute-start | bytes 1572872 | tf_op jit(solution)/shard_map/ppermute | solution.py:16
  59.0 10.7 %collective-permute-done.4 = bf16[2,128,1024]{2,1,0:T(8,128)(2,1)S(1)} collective-permute-done((bf16[2,128,1024]{2,1,0:T(8,128)(2,1)S(1)}, bf16[2,128,1024]{2,1,0:T(8,128)(2,1)S(1)}, u32[]{:S(2)}, u32[]{:S(2)}) %collective-permute-start.4) | collective-permute-done | bytes 524320 | tf_op jit(solution)/shard_map/ppermute | solution.py:16
  69.8 1.9 collective-permute-start.5
  71.7 0.3 multiply_cosine_fusion
  72.0 0.3 subtract_convert_fusion
  72.5 12.6 %collective-permute-done.5 = bf16[2,128,1024]{2,1,0:T(8,128)(2,1)S(1)} collective-permute-done((bf16[2,128,1024]{2,1,0:T(8,128)(2,1)S(1)}, bf16[2,128,1024]{2,1,0:T(8,128)(2,1)S(1)}, u32[]{:S(2)}, u32[]{:S(2)}) %collective-permute-start.5) | collective-permute-done | bytes 524320 | tf_op jit(solution)/shard_map/ppermute | solution.py:16
  85.2 1.4 convolution_convert_fusion
  86.7 0.5 fusion
  87.2 1.9 collective-permute-start
  89.3 24.6 %reduce-scatter.3.cloned.1.call-done = bf16[16,512]{1,0:T(8,128)(2,1)} async-done(((bf16[128,512]{1,0:T(8,128)(2,1)}), bf16[16,512]{1,0:T(8,128)(2,1)}) %reduce-scatter.3.cloned.1.call-update) | async-done | bytes 16400 | tf_op jit(solution)/shard_map/reduce_scatter | solution.py:44
  113.9 0.7 reshape.207
  114.7 0.7 pad_maximum_fusion.2
  115.4 0.7 slice_bitcast_fusion.2
  116.2 108.4 %reduce-scatter.5.cloned.1.call-done = bf16[256,512]{1,0:T(8,128)(2,1)} async-done(((bf16[1024,512]{1,0:T(8,128)(2,1)}), bf16[256,512]{1,0:T(8,128)(2,1)}) %reduce-scatter.5.cloned.1.call-update) | async-done | bytes 262160 | tf_op jit(solution)/shard_map/reduce_scatter | solution.py:72
  224.6 1.7 broadcast_in_dim_reshape.3
  226.3 0.7 copy.30
  (31 shorter events, 1.0 us)
Async XLA Ops:
  7.2 5.0 %copy-start = (bf16[1,1,128,1024]{3,2,1,0:T(8,128)(2,1)S(1)}, bf16[1,1,128,1024]{3,2,1,0:T(8,128)(2,1)}, u32[]{:S(2)}) copy-start(bf16[1,1,128,1024]{3,2,1,0:T(8,128)(2,1)} %param.10) | copy-start | bytes 786436
  7.2 5.0 %copy-start.1 = (bf16[1,1,128,1024]{3,2,1,0:T(8,128)(2,1)S(1)}, bf16[1,1,128,1024]{3,2,1,0:T(8,128)(2,1)}, u32[]{:S(2)}) copy-start(bf16[1,1,128,1024]{3,2,1,0:T(8,128)(2,1)} %param.7) | copy-start | bytes 786436
  7.2 3.1 %copy-start.4 = (s32[32]{0:T(128)S(1)}, s32[32]{0:T(128)}, u32[]{:S(2)}) copy-start(s32[32]{0:T(128)} %param.11) | copy-start | bytes 388
  7.2 106.7 %reduce-scatter.3.cloned.1.call-start = ((), (), s32[]{:S(2)}) async-start(), calls=%async_computation.2 | async-start | bytes 147456 | tf_op jit(solution)/shard_map/reduce_scatter | solution.py:44
  8.4 3.8 %collective-permute-start.1 = (bf16[2,128,1024]{2,1,0:T(8,128)(2,1)S(1)}, bf16[2,128,1024]{2,1,0:T(8,128)(2,1)S(1)}, u32[]{:S(2)}, u32[]{:S(2)}) collective-permute-start(bf16[2,128,1024]{2,1,0:T(8,128)(2,1)S(1)} %pad_maximum_fusion), channel_id=1, source_target_pairs={{0,32},{32,0},{64,96},{96,64},{128,160},{160,128},{192,224},{224,1... | collective-permute-start | bytes 1572872 | tf_op jit(solution)/shard_map/ppermute | solution.py:16
  12.3 15.9 %collective-permute-start.2 = (bf16[2,128,1024]{2,1,0:T(8,128)(2,1)S(1)}, bf16[2,128,1024]{2,1,0:T(8,128)(2,1)S(1)}, u32[]{:S(2)}, u32[]{:S(2)}) collective-permute-start(bf16[2,128,1024]{2,1,0:T(8,128)(2,1)S(1)} %broadcast_select_fusion), channel_id=1, source_target_pairs={{0,64},{32,96},{64,0},{96,32},{128,192},{160,224},{192,128},{224,1... | collective-permute-start | bytes 1572872 | tf_op jit(solution)/shard_map/ppermute | solution.py:16
  28.1 4.4 %copy-start.3 = (bf16[1,1024,4,128]{3,2,1,0:T(4,128)(2,1)S(1)}, bf16[1,1024,4,128]{3,2,1,0:T(4,128)(2,1)}, u32[]{:S(2)}) copy-start(bf16[1,1024,4,128]{3,2,1,0:T(4,128)(2,1)} %param.9) | copy-start | bytes 3145732
  28.2 16.6 %collective-permute-start.3 = (bf16[2,128,1024]{2,1,0:T(8,128)(2,1)S(1)}, bf16[2,128,1024]{2,1,0:T(8,128)(2,1)S(1)}, u32[]{:S(2)}, u32[]{:S(2)}) collective-permute-start(bf16[2,128,1024]{2,1,0:T(8,128)(2,1)S(1)} %broadcast_select_fusion.1), channel_id=1, source_target_pairs={{0,128},{32,160},{64,192},{96,224},{128,0},{160,32},{192,64},{224,... | collective-permute-start | bytes 1572872 | tf_op jit(solution)/shard_map/ppermute | solution.py:16
  33.5 25.5 %copy-start.5 = (s32[1,1,128]{2,1,0:T(1,128)S(1)}, s32[1,1,128]{2,1,0:T(1,128)}, u32[]{:S(2)}) copy-start(s32[1,1,128]{2,1,0:T(1,128)} %param.13) | copy-start | bytes 1540
  33.5 25.5 %copy-start.2 = (bf16[1,1,128,4,128]{4,3,2,1,0:T(4,128)(2,1)S(1)}, bf16[1,1,128,4,128]{4,3,2,1,0:T(4,128)(2,1)}, u32[]{:S(2)}) copy-start(bf16[1,1,128,4,128]{4,3,2,1,0:T(4,128)(2,1)} %param.12) | copy-start | bytes 393220
  33.5 191.0 %reduce-scatter.5.cloned.1.call-start = ((), (), s32[]{:S(2)}) async-start(), calls=%async_computation.3 | async-start | bytes 1310720 | tf_op jit(solution)/shard_map/reduce_scatter | solution.py:72
  44.9 24.8 %collective-permute-start.4 = (bf16[2,128,1024]{2,1,0:T(8,128)(2,1)S(1)}, bf16[2,128,1024]{2,1,0:T(8,128)(2,1)S(1)}, u32[]{:S(2)}, u32[]{:S(2)}) collective-permute-start(bf16[2,128,1024]{2,1,0:T(8,128)(2,1)S(1)} %broadcast_select_fusion.2), channel_id=1, source_target_pairs={{0,256},{32,288},{64,320},{96,352},{128,384},{160,416},{192,448},{... | collective-permute-start | bytes 1572872 | tf_op jit(solution)/shard_map/ppermute | solution.py:16
  69.8 15.4 %collective-permute-start.5 = (bf16[2,128,1024]{2,1,0:T(8,128)(2,1)S(1)}, bf16[2,128,1024]{2,1,0:T(8,128)(2,1)S(1)}, u32[]{:S(2)}, u32[]{:S(2)}) collective-permute-start(bf16[2,128,1024]{2,1,0:T(8,128)(2,1)S(1)} %broadcast_select_fusion.3), channel_id=1, source_target_pairs={{0,512},{32,544},{64,576},{96,608},{128,640},{160,672},{192,704},{... | collective-permute-start | bytes 1572872 | tf_op jit(solution)/shard_map/ppermute | solution.py:16
  86.7 2.5 %copy-start.6 = (s32[1,1,128]{2,1,0:T(1,128)S(1)}, s32[1,1,128]{2,1,0:T(1,128)}, u32[]{:S(2)}) copy-start(s32[1,1,128]{2,1,0:T(1,128)} %param.8) | copy-start | bytes 1540
  87.2 27.5 %collective-permute-start = (bf16[1,1,128,1024]{3,2,1,0:T(8,128)(2,1)S(1)}, bf16[1,1,128,1024]{3,2,1,0:T(8,128)(2,1)S(1)}, u32[]{:S(2)}, u32[]{:S(2)}) collective-permute-start(bf16[1,1,128,1024]{3,2,1,0:T(8,128)(2,1)S(1)} %fusion), channel_id=1, source_target_pairs={{32,0},{64,32},{96,64},{128,96},{160,128},{192,160},{224,192},{256... | collective-permute-start | bytes 786440 | tf_op jit(solution)/shard_map/ppermute | solution.py:12
Sparse Core Ops, SparseCore 0:
  33.7 80.1 reduce-scatter.2
  117.3 107.1 reduce-scatter.4
where the time goes:
time: 234 us
  waiting for transfers between devices  183 us (78%)
  starting transfers between devices  26.6 us (11%)
  between operations  14.4 us (6%)
  local copies, waits for them, and re-layouts  3.9 us (2%)
  other arithmetic  3.23 us (1%)
  matrix products  2.89 us (1%)
    reduce_scatter x1, waiting for transfers between devices, body(): lax.psum_scatter(jnp.einsum('rd,rn->dn', held, grad_flat, preferred_eleme...  108 us
    ppermute x5, waiting for transfers between devices, swapped_2(): lax.ppermute(value, axis, [(i, i ^ 1 << distance) for i in range(lax.axis...  49.7 us
    ppermute x5, starting transfers between devices, swapped_2(): lax.ppermute(value, axis, [(i, i ^ 1 << distance) for i in range(lax.axis...  24.6 us
    reduce_scatter x1, waiting for transfers between devices, body(): lax.psum_scatter(jnp.dot(inputs, flat_weight, preferred_element_type=jnp....  24.6 us
  transfers between devices with their start and end apart: 8, of which 7 were waited for; matrix products, arithmetic and copies ran while one was open for 3% of the time, Pallas kernels for 0%

commit v1 on v0

v1 whole, which is shorter than its diff:
```python
import functools

import jax
import jax.numpy as jnp
from jax import lax
from jax.experimental import pallas as pl
from jax.experimental.pallas import tpu as pltpu
from jax.sharding import PartitionSpec as P

THETA = 500000.0
MESH = pl.DeviceIdType.MESH
QUAD = 4


def rope_tables(positions, head_size):
    half = head_size // 2
    freqs = THETA ** (-(2.0 * jnp.arange(half, dtype=jnp.float32)) / head_size)
    angles = positions.astype(jnp.float32)[..., None] * freqs
    return (jnp.cos(angles), jnp.sin(angles))


def rotate(keys, cosine, sine, sign):
    half = keys.shape[-1] // 2
    first = keys[..., :half]
    second = keys[..., half:]
    return jnp.concatenate(
        [first * cosine - sign * second * sine, second * cosine + sign * first * sine], axis=-1
    )


def exchange_kernel(
    mask, sizes, fwd, stash, grad, partial, g,
    evicted, grad_in, held, g_all, keys,
    s_send, s_recv, h_send, h_recv, k_send, k_recv, c_send, c_recv, a_send, g_recv, far_ready,
):
    n_s, n_t, n_p = sizes
    n_z = n_t * n_p
    s = lax.axis_index("section")
    t = lax.axis_index("tensor")
    p = lax.axis_index("dp")
    z = p * n_t + t
    partner = s
    for bit in range(n_s.bit_length() - 1):
        if mask >> bit & 1:
            partner = partner + (1 << bit) * (1 - 2 * ((s // (1 << bit)) % 2))
    before = (s + n_s - 1) % n_s
    after = (s + 1) % n_s

    def dp(step):
        return (p + step + n_p) % n_p

    def along(step):
        there = (z + step + n_z) % n_z
        return (s, there % n_t, there // n_t)

    def device(a):
        return {"section": a[0], "tensor": a[1], "dp": a[2]}

    def remote(src, dst, send, recv, a):
        return pltpu.make_async_remote_copy(
            src_ref=src, dst_ref=dst, send_sem=send, recv_sem=recv,
            device_id=device(a), device_id_type=MESH,
        )

    half = (t // QUAD) % 2
    way = 1 - 2 * half
    r = t % QUAD

    peers = [(partner, t, p), (partner, t, dp(1)), (partner, t, dp(-1))]
    peers += [(s, t, dp(1)), (s, t, dp(-1)), along(QUAD), along(-QUAD)]
    peers += [(s, (t + j) % n_t, p) for j in range(1, n_t)]
    barrier = pltpu.get_barrier_semaphore()
    for a in peers + [(before, t, p), (after, t, p)]:
        pl.semaphore_signal(barrier, inc=1, device_id=device(a), device_id_type=MESH)
    pl.semaphore_wait(barrier, len(peers) + 2)

    pl.semaphore_signal(far_ready, inc=1, device_id=device((s, t, dp(-1))), device_id_type=MESH)

    rows = g.shape[0] // QUAD
    mine = pl.ds(pl.multiple_of(r * rows, rows), rows)
    q_near = (p - way + n_p) % n_p
    q_far = (p + way + n_p) % n_p
    q_last = (p + n_p // 2) % n_p

    def step(q, src, slot, to):
        return remote(src, g_all.at[q, mine], c_send.at[slot], g_recv.at[q, r], along(to * QUAD))

    def spread(q, slot):
        copies = []
        for j in range(1, QUAD):
            there = half * QUAD + (r + j) % QUAD
            copies.append(
                remote(
                    g_all.at[q, mine], g_all.at[q, mine], a_send.at[slot, j], g_recv.at[q, r],
                    (s, there, p),
                )
            )
            copies[-1].start()
        return copies

    def arrived(q, block):
        part = g_all.at[q, pl.ds(pl.multiple_of(block * rows, rows), rows)]
        remote(part, part, c_send.at[0], g_recv.at[q, block], (s, t, p)).wait_recv()

    sent = [step(p, g.at[mine], 0, -way)]
    sent[0].start()

    def key_copy(j):
        there = (t + j) % n_t
        block = partial.shape[0] // n_t
        return remote(
            partial.at[pl.ds(pl.multiple_of(there * block, block), block)], keys.at[t],
            k_send.at[j], k_recv.at[t], (s, there, p),
        )

    def held_copy(j):
        there = dp(j)
        width = stash.shape[1] // n_p
        return remote(
            stash.at[:, pl.ds(pl.multiple_of(there * width, width), width)], held.at[p],
            h_send.at[j], h_recv.at[p], (partner, t, there),
        )

    def go(copy):
        copy.start()
        sent.append(copy)

    for j in range(1, n_t):
        go(key_copy(j))
    go(held_copy(1))
    go(held_copy(3))
    go(held_copy(0))
    go(remote(fwd, evicted, s_send.at[0], s_recv.at[0], (partner, t, p)))
    go(remote(grad, grad_in, s_send.at[1], s_recv.at[1], (before, t, p)))

    arrived(q_near, r)
    go(step(q_near, g_all.at[q_near, mine], 1, way))
    sent += spread(q_near, 0)
    arrived(q_far, r)
    go(step(q_far, g_all.at[q_far, mine], 2, -way))
    sent += spread(q_far, 1)
    pl.semaphore_wait(far_ready, 1)
    go(held_copy(2))
    arrived(q_last, r)
    sent += spread(q_last, 2)

    for q in (q_near, q_far, q_last):
        for j in range(1, QUAD):
            arrived(q, (r + j) % QUAD)
    for j in range(1, n_t):
        block = keys.at[(t + j) % n_t]
        remote(block, block, k_send.at[j], k_recv.at[(t + j) % n_t], (s, t, p)).wait_recv()
    for j in range(n_p):
        block = held.at[dp(j)]
        remote(block, block, h_send.at[j], h_recv.at[dp(j)], (s, t, p)).wait_recv()
    remote(fwd, evicted, s_send.at[0], s_recv.at[0], (partner, t, p)).wait_recv()
    remote(grad, grad_in, s_send.at[1], s_recv.at[1], (before, t, p)).wait_recv()
    for copy in sent:
        copy.wait_send()


def exchange(mask, sizes, fwd, stash, grad, partial, g):
    n_s, n_t, n_p = sizes
    dtype = fwd.dtype
    tokens, width = fwd.shape
    columns = g.shape[1]
    dma = pltpu.SemaphoreType.DMA
    anywhere = pl.BlockSpec(memory_space=pl.ANY)
    shapes = [
        (tokens, width), (tokens, width), (n_p, tokens, width // n_p), (n_p, tokens, columns),
        (n_t, tokens // n_t, columns),
    ]
    return pl.pallas_call(
        functools.partial(exchange_kernel, mask, sizes),
        out_shape=[jax.ShapeDtypeStruct(shape, dtype) for shape in shapes],
        in_specs=[anywhere] * 5,
        out_specs=[anywhere] * 5,
        scratch_shapes=[
            dma((2,)), dma((2,)), dma((n_p,)), dma((n_p,)), dma((n_t,)), dma((n_t,)),
            dma((3,)), dma((n_p, QUAD)), dma((3, QUAD)), dma((n_p, QUAD)),
            pltpu.SemaphoreType.REGULAR,
        ],
        compiler_params=pltpu.CompilerParams(collective_id=mask % (n_s // 2), has_side_effects=True),
        name=f"exchange_{mask}",
    )(fwd, stash, grad, partial, g)


def body(sizes, fwd_input, fwd_positions, key_weight, stash, partner, key_grad, bwd_positions):
    n_s, n_t, n_p = sizes
    inputs = fwd_input[0, 0]
    weight = key_weight[0]
    width_local, head_count, head_size = weight.shape
    columns = head_count * head_size
    flat_weight = weight.reshape(width_local, columns)
    tokens = inputs.shape[0]
    my_rows = tokens // n_t
    partial = jnp.dot(inputs, flat_weight, preferred_element_type=jnp.float32).astype(jnp.bfloat16)
    grads = key_grad[0, 0].astype(jnp.float32)
    back_cos, back_sin = rope_tables(bwd_positions[0, 0], head_size)
    grad_pre = rotate(grads, back_cos[:, None], back_sin[:, None], -1.0).astype(jnp.bfloat16)
    g = grad_pre.reshape(tokens, columns)
    input_grad = jnp.einsum("rn,dn->rd", g, flat_weight, preferred_element_type=jnp.float32)
    input_grad = input_grad.astype(jnp.bfloat16)

    first_mask = n_s // 2
    branches = [
        functools.partial(exchange, mask, sizes) for mask in range(first_mask, 2 * first_mask)
    ]
    evicted, grad_in, held, g_all, keys = lax.switch(
        partner[0] - first_mask, branches, inputs, stash[0, 0], input_grad, partial, g
    )

    me_t = lax.axis_index("tensor")
    me_p = lax.axis_index("dp")
    row_start = me_t * my_rows
    own = lax.dynamic_slice_in_dim(partial, row_start, my_rows, 0)
    is_own = (jnp.arange(n_t, dtype=jnp.int32) == me_t)[:, None, None]
    summed = jnp.sum(jnp.where(is_own, own[None], keys).astype(jnp.float32), axis=0)
    summed = summed.reshape(my_rows, head_count, head_size)
    my_positions = lax.dynamic_slice_in_dim(fwd_positions[0, 0], row_start, my_rows, 0)
    cosine, sine = rope_tables(my_positions, head_size)
    key_out = rotate(summed, cosine[:, None], sine[:, None], 1.0).astype(jnp.bfloat16)

    g_all = lax.dynamic_update_slice_in_dim(g_all, g[None], me_p, 0)
    weight_grad = jnp.einsum("prd,prn->dn", held, g_all, preferred_element_type=jnp.float32)
    weight_grad = weight_grad.astype(jnp.bfloat16).reshape(-1, head_count, head_size)
    return key_out[None, None], grad_in[None, None], evicted[None, None], weight_grad[None]


def solution(mesh):
    sizes = (mesh.shape["section"], mesh.shape["tensor"], mesh.shape["dp"])
    placed = (
        P("dp", "section", None, "tensor"),
        P("dp", "section", None),
        P("section", "tensor", None, None),
        P("dp", "section", None, "tensor"),
        P(),
        P("dp", "section", None, None, None),
        P("dp", "section", None),
    )
    return jax.shard_map(
        functools.partial(body, sizes),
        mesh=mesh,
        in_specs=placed,
        out_specs=(
            P("dp", "section", "tensor", None, None),
            P("dp", "section", None, "tensor"),
            P("dp", "section", None, "tensor"),
            P("section", ("tensor", "dp"), None, None),
        ),
        check_vma=False,
    )
```

time: 234 us -> 79.4 us (0.34)
  the two profiles are of different devices: /device:TPU:10 before, /device:TPU:38 now
where the time goes in v1:
time: 79.4 us; the launch traced here: 80.2 us
  Pallas kernels  71 us (89%)
  local copies, waits for them, and re-layouts  5.3 us (7%)
  other arithmetic  1.89 us (2%)
  matrix products  1.11 us (1%)
  between operations  0.86 us (1%)
    pallas_call x1, Pallas kernels, exchange(): pl.pallas_call(functools.partial(exchange_kernel, mask, sizes), out_shape...  71 us
    unnamed x16, local copies, waits for them, and re-layouts  3.76 us

profile of v1, /device:TPU:38, one launch (start us, length us, event | category | flops | bytes accessed | tf_op | source)
XLA Modules:
  0.0 80.2 jit_solution(4406523040329243683)
XLA Ops:
  0.7 0.6 copy-done.4
  1.3 0.3 multiply_cosine_fusion
  1.7 0.3 multiply_subtract_fusion
  1.9 0.2 pad_maximum_fusion
  2.1 0.0 copy-start.1
  2.2 0.5 convolution_convert_fusion
  2.6 0.5 copy-done.1
  3.1 0.3 convolution_convert_fusion.1
  3.4 0.0 copy-start.5
  3.4 0.6 copy-done.5
  4.1 71.7 %conditional.1 = (bf16[4,128,256]{2,1,0:T(8,128)(2,1)S(1)}, bf16[4,128,512]{2,1,0:T(8,128)(2,1)S(1)}, bf16[8,16,512]{2,1,0:T(8,128)(2,1)S(1)}, bf16[1,1,128,1024...) conditional(s32[]{:T(128)} %bitcast.49, ...), branch_computations={%region_0.0_spmd, %region_1.0_spmd, %region_2.0_spmd, %region_3.0_... | conditional | bytes 262184 | solution.py:209
  4.2 0.7 copy.81
  4.8 71.0 %exchange_22.1 = (bf16[128,1024]{1,0:T(8,128)(2,1)S(1)}, bf16[128,1024]{1,0:T(8,128)(2,1)S(1)}, bf16[4,128,256]{2,1,0:T(8,128)(2,1)S(1)}, bf16[4,128,512]{2,1,0:T(8,128)(2,1)S(1)}, bf16[8,16,512]{2,1,0:T(8,128)(2,1)S(1)}) custom-call(bf16[128,1024]{1,0:T(8,128)(2,1)S(1)} %get-tuple-element.326.fwd, bf16[128,1024]{1,0:T(8,128)(2,1)S(1)} %bitcast.151, ...), custom_call_target="tpu_custom_call" | custom-call | tf_op jit(solution)/shard_map/cond/branch_6_fun/exchange_22/pallas_call | solution.py:173
  75.8 0.1 convert_element_type.176
  75.9 0.3 fusion
  76.3 0.8 broadcast_in_dim_reshape.4
  77.0 0.1 convert_reduce_fusion
  77.2 0.6 copy-done.6
  77.8 0.1 fusion.11
  77.9 0.1 multiply_cosine_fusion.1
  78.0 0.1 fusion.8
  78.1 0.7 pad_maximum_fusion.1
  78.8 0.7 copy.174
  79.5 0.7 copy.175
  (15 shorter events, 0.1 us)
Async XLA Ops:
  0.6 0.7 copy-start.4
  0.6 1.0 %copy-start.2 = (bf16[1,1,128,4,128]{4,3,2,1,0:T(4,128)(2,1)S(1)}, bf16[1,1,128,4,128]{4,3,2,1,0:T(4,128)(2,1)}, u32[]{:S(2)}) copy-start(bf16[1,1,128,4,128]{4,3,2,1,0:T(4,128)(2,1)} %param.28) | copy-start | bytes 393220
  0.7 1.5 %copy-start.3 = (bf16[1,1024,4,128]{3,2,1,0:T(4,128)(2,1)S(1)}, bf16[1,1024,4,128]{3,2,1,0:T(4,128)(2,1)}, u32[]{:S(2)}) copy-start(bf16[1,1024,4,128]{3,2,1,0:T(4,128)(2,1)} %param.25) | copy-start | bytes 3145732
  2.1 1.0 %copy-start.1 = (bf16[1,1,128,1024]{3,2,1,0:T(8,128)(2,1)S(1)}, bf16[1,1,128,1024]{3,2,1,0:T(8,128)(2,1)}, u32[]{:S(2)}) copy-start(bf16[1,1,128,1024]{3,2,1,0:T(8,128)(2,1)} %param.23) | copy-start | bytes 786436
  3.1 1.0 %copy-start = (bf16[1,1,128,1024]{3,2,1,0:T(8,128)(2,1)S(1)}, bf16[1,1,128,1024]{3,2,1,0:T(8,128)(2,1)}, u32[]{:S(2)}) copy-start(bf16[1,1,128,1024]{3,2,1,0:T(8,128)(2,1)} %param.26) | copy-start | bytes 786436
  3.4 0.7 copy-start.5
  77.1 0.7 copy-start.6

commit v2 on v1

v2 whole, which is shorter than its diff:
```python
import functools

import jax
import jax.numpy as jnp
from jax import lax
from jax.experimental import pallas as pl
from jax.experimental.pallas import tpu as pltpu
from jax.sharding import PartitionSpec as P

THETA = 500000.0
MESH = pl.DeviceIdType.MESH
QUAD = 4


def rope_tables(positions, head_size):
    half = head_size // 2
    freqs = THETA ** (-(2.0 * jnp.arange(half, dtype=jnp.float32)) / head_size)
    angles = positions.astype(jnp.float32)[..., None] * freqs
    return (jnp.cos(angles), jnp.sin(angles))


def rotate(keys, cosine, sine, sign):
    half = keys.shape[-1] // 2
    first = keys[..., :half]
    second = keys[..., half:]
    return jnp.concatenate(
        [first * cosine - sign * second * sine, second * cosine + sign * first * sine], axis=-1
    )


def exchange_kernel(
    mask, sizes, fwd, stash, grad, partial, g,
    evicted, grad_in, held, g_all, keys,
    k_parts, k_sum,
    s_send, s_recv, h_send, h_recv, k_send, k_recv, c_send, c_recv, own_sem, own_g_sem, near_ready, pair_ready,
    far_ready, last_ready,
):
    n_s, n_t, n_p = sizes
    n_z = n_t * n_p
    s = lax.axis_index("section")
    t = lax.axis_index("tensor")
    p = lax.axis_index("dp")
    z = p * n_t + t
    partner = s
    for bit in range(n_s.bit_length() - 1):
        if mask >> bit & 1:
            partner = partner + (1 << bit) * (1 - 2 * ((s // (1 << bit)) % 2))
    before = (s + n_s - 1) % n_s
    after = (s + 1) % n_s
    half = (t // QUAD) % 2
    way = 1 - 2 * half
    r = t % QUAD

    def dp(step):
        return (p + step + n_p) % n_p

    def along(step):
        there = (z + step + n_z) % n_z
        return (s, there % n_t, there // n_t)

    def mate(j):
        return (s, half * QUAD + (r + j) % QUAD, p)

    def device(a):
        return {"section": a[0], "tensor": a[1], "dp": a[2]}

    def signal(sem, a):
        pl.semaphore_signal(sem, inc=1, device_id=device(a), device_id_type=MESH)

    def remote(src, dst, send, recv, a):
        return pltpu.make_async_remote_copy(
            src_ref=src, dst_ref=dst, send_sem=send, recv_sem=recv,
            device_id=device(a), device_id_type=MESH,
        )

    peers = [(partner, t, p), (before, t, p), (after, t, p)]
    peers += [along(j) for j in (-QUAD, QUAD, -2, 2, -1, 1)]
    peers += [mate(j) for j in range(1, QUAD)]
    barrier = pltpu.get_barrier_semaphore()
    for a in peers:
        signal(barrier, a)
    block = k_sum.shape[1]
    own_part = pltpu.make_async_copy(partial.at[:, r], k_parts.at[0], own_sem)
    own_part.start()
    own_g = pltpu.make_async_copy(g, g_all.at[p], own_g_sem)
    own_g.start()
    pl.semaphore_wait(barrier, len(peers))

    sent = []

    def go(copy, when=None):
        if when is None:
            copy.start()
        else:
            pl.when(when)(copy.start)
        sent.append((copy, when))

    signal(near_ready, along(QUAD))
    signal(near_ready, along(-QUAD))

    rows = g.shape[0] // QUAD
    base = pl.multiple_of(r * rows, rows)
    q_near = (p - way + n_p) % n_p
    q_far = (p + way + n_p) % n_p
    q_last = (p + n_p // 2) % n_p

    def piece(src, q, slot, there, start, size, i):
        at = pl.ds(start, size)
        return remote(src.at[at], g_all.at[q, at], c_send.at[slot, i], c_recv.at[q, i], there)

    def step(src, q, slot, to):
        return piece(src, q, slot, along(to * QUAD), base, rows, 0)

    def spread(src, q, slot):
        small = rows // 2
        plans = ((1, 0, rows, 1), (-1, 0, rows, 2), (2, 0, small, 3), (-2, small, small, 4))
        for to, offset, size, i in plans:
            there = along(to)
            start = pl.multiple_of(base + offset, small)
            go(piece(src, q, slot, there, start, size, i), there[2] != q)

    def arrived(q, i):
        small = rows // 2
        back, offset, size = ((0, 0, rows), (1, 0, rows), (-1, 0, rows), (2, 0, small), (-2, small, small))[i]
        start = pl.multiple_of(((r - back + QUAD) % QUAD) * rows + offset, small)
        piece(g_all.at[q], q, 0, (s, t, p), start, size, i).wait_recv()

    go(step(g, p, 0, -way))
    spread(g, p, 0)
    for j in range(1, QUAD):
        go(remote(partial.at[:, (r + j) % QUAD], k_parts.at[QUAD - j], k_send.at[j], k_recv.at[QUAD - j], mate(j)))

    def held_copy(j):
        there = dp(j)
        width = stash.shape[1] // n_p
        return remote(
            stash.at[:, pl.ds(pl.multiple_of(there * width, width), width)], held.at[p],
            h_send.at[j], h_recv.at[p], (partner, t, there),
        )

    pl.semaphore_wait(near_ready, 2)
    signal(pair_ready, (partner, t, p))
    signal(far_ready, (s, t, dp(-1)))

    arrived(q_near, 0)
    go(step(g_all.at[q_near], q_near, 1, way))
    spread(g_all.at[q_near], q_near, 1)

    pl.semaphore_wait(pair_ready, 1)
    go(held_copy(1))
    go(held_copy(3))
    go(held_copy(0))
    go(remote(fwd, evicted, s_send.at[0], s_recv.at[0], (partner, t, p)))
    go(remote(grad, grad_in, s_send.at[1], s_recv.at[1], (before, t, p)))

    own_part.wait()
    for j in range(1, QUAD):
        remote(k_parts.at[j], k_parts.at[j], k_send.at[j], k_recv.at[j], (s, t, p)).wait_recv()
    total = k_parts[0].astype(jnp.float32)
    for j in range(1, QUAD):
        total = total + k_parts[j].astype(jnp.float32)
    k_sum[...] = total.astype(k_sum.dtype)

    pl.semaphore_wait(far_ready, 1)
    signal(last_ready, (partner, t, p))
    arrived(q_far, 0)
    go(step(g_all.at[q_far], q_far, 2, -way))
    spread(g_all.at[q_far], q_far, 2)
    own_keys = pltpu.make_async_copy(k_sum.at[half], keys.at[0], own_sem)
    own_keys.start()
    go(remote(k_sum.at[1 - half], keys.at[1], k_send.at[0], k_recv.at[0], along(way * QUAD)))

    pl.semaphore_wait(last_ready, 1)
    go(held_copy(2))
    arrived(q_last, 0)
    spread(g_all.at[q_last], q_last, 3)

    for q in (q_near, q_far, q_last):
        for i in range(1, 5):
            arrived(q, i)
    own_g.wait()
    own_keys.wait()
    remote(k_sum.at[0], keys.at[1], k_send.at[0], k_recv.at[0], (s, t, p)).wait_recv()
    for j in range(n_p):
        part = held.at[dp(j)]
        remote(part, part, h_send.at[j], h_recv.at[dp(j)], (s, t, p)).wait_recv()
    remote(fwd, evicted, s_send.at[0], s_recv.at[0], (partner, t, p)).wait_recv()
    remote(grad, grad_in, s_send.at[1], s_recv.at[1], (before, t, p)).wait_recv()
    for copy, when in sent:
        if when is None:
            copy.wait_send()
        else:
            pl.when(when)(copy.wait_send)


def exchange(mask, sizes, fwd, stash, grad, partial, g):
    n_s, n_t, n_p = sizes
    dtype = fwd.dtype
    tokens, width = fwd.shape
    columns = partial.shape[1]
    block = tokens // n_t
    dma = pltpu.SemaphoreType.DMA
    anywhere = pl.BlockSpec(memory_space=pl.ANY)
    shapes = [
        (tokens, width), (tokens, width), (n_p, tokens, width // n_p), (n_p, *g.shape),
        (2, block, columns),
    ]
    return pl.pallas_call(
        functools.partial(exchange_kernel, mask, sizes),
        out_shape=[jax.ShapeDtypeStruct(shape, dtype) for shape in shapes],
        in_specs=[anywhere] * 5,
        out_specs=[anywhere] * 5,
        scratch_shapes=[
            pltpu.VMEM((QUAD, 2, block, columns), dtype),
            pltpu.VMEM((2, block, columns), dtype),
            dma((2,)), dma((2,)), dma((n_p,)), dma((n_p,)), dma((QUAD,)), dma((QUAD,)),
            dma((4, 5)), dma((n_p, 5)), dma, dma,
        ] + [pltpu.SemaphoreType.REGULAR] * 4,
        compiler_params=pltpu.CompilerParams(collective_id=mask % (n_s // 2), has_side_effects=True),
        name=f"exchange_{mask}",
    )(fwd, stash, grad, partial.reshape(2, QUAD, block, columns), g)


def finish_kernel(
    evicted, grad_in, held, g_all, keys, positions, freqs,
    evicted_out, grad_out, key_out, weight_out, k_buffer, w_buffer, at_buffer, angles, sems,
):
    copies = [
        pltpu.make_async_copy(evicted, evicted_out, sems.at[0]),
        pltpu.make_async_copy(grad_in, grad_out, sems.at[1]),
    ]
    for copy in copies:
        copy.start()
    fetch = pltpu.make_async_copy(positions, at_buffer, sems.at[4])
    fetch.start()
    total = None
    for q in range(held.shape[0]):
        one = lax.dot_general(
            held[q], g_all[q], (((0,), (0,)), ((), ())), preferred_element_type=jnp.float32
        )
        total = one if total is None else total + one
    w_buffer[...] = total.reshape(w_buffer.shape).astype(w_buffer.dtype)
    copies.append(pltpu.make_async_copy(w_buffer, weight_out, sems.at[3]))
    copies[-1].start()

    rows, heads, size = k_buffer.shape
    fetch.wait()
    tokens = at_buffer.shape[1]
    spread = jnp.broadcast_to(at_buffer[...].astype(jnp.float32), (size, tokens))
    angles[...] = spread.T * freqs[...]
    start = pl.multiple_of(lax.axis_index("tensor") * rows, rows)
    mine = angles[pl.ds(start, rows), :]
    upper = lax.broadcasted_iota(jnp.int32, mine.shape, 1) >= size // 2
    cosine, sine = jnp.cos(mine), jnp.sin(mine)
    sine = jnp.where(upper, sine, -sine)
    summed = keys[0].astype(jnp.float32) + keys[1].astype(jnp.float32)
    turned = []
    for h in range(heads):
        x = summed[:, h * size : (h + 1) * size]
        turned.append(x * cosine + pltpu.roll(x, size // 2, 1) * sine)
    turned = jnp.concatenate(turned, axis=1)
    k_buffer[...] = turned.reshape(k_buffer.shape).astype(k_buffer.dtype)
    copies.append(pltpu.make_async_copy(k_buffer, key_out, sems.at[2]))
    copies[-1].start()
    for copy in copies:
        copy.wait()


def finish(heads, size, evicted, grad_in, held, g_all, keys, positions):
    half = size // 2
    freqs = THETA ** (-(2.0 * jnp.arange(half, dtype=jnp.float32)) / size)
    freqs = jnp.concatenate([freqs, freqs])[None]
    anywhere = pl.BlockSpec(memory_space=pl.ANY)
    vmem = pl.BlockSpec(memory_space=pltpu.VMEM)
    dtype = evicted.dtype
    k_shape = (keys.shape[1], heads, size)
    w_shape = (held.shape[2], heads, size)
    shapes = (evicted.shape, grad_in.shape, k_shape, w_shape)
    return pl.pallas_call(
        finish_kernel,
        out_shape=[jax.ShapeDtypeStruct(shape, dtype) for shape in shapes],
        in_specs=[anywhere] * 2 + [vmem] * 3 + [anywhere, vmem],
        out_specs=[anywhere] * 4,
        scratch_shapes=[
            pltpu.VMEM(k_shape, dtype), pltpu.VMEM(w_shape, dtype),
            pltpu.VMEM(positions.shape, jnp.int32), pltpu.VMEM((positions.shape[1], size), jnp.float32),
            pltpu.SemaphoreType.DMA((5,)),
        ],
        name="finish",
    )(evicted, grad_in, held, g_all, keys, positions, freqs)


def body(sizes, fwd_input, fwd_positions, key_weight, stash, partner, key_grad, bwd_positions):
    n_s, n_t, n_p = sizes
    inputs = fwd_input[0, 0]
    weight = key_weight[0]
    width_local, head_count, head_size = weight.shape
    columns = head_count * head_size
    flat_weight = weight.reshape(width_local, columns)
    tokens = inputs.shape[0]
    partial = jnp.dot(inputs, flat_weight, preferred_element_type=jnp.float32).astype(jnp.bfloat16)
    grads = key_grad[0, 0].astype(jnp.float32)
    back_cos, back_sin = rope_tables(bwd_positions[0, 0], head_size)
    g = rotate(grads, back_cos[:, None], back_sin[:, None], -1.0).astype(jnp.bfloat16)
    flat_g = g.reshape(tokens, columns)
    input_grad = jnp.einsum("rn,dn->rd", flat_g, flat_weight, preferred_element_type=jnp.float32)
    input_grad = input_grad.astype(jnp.bfloat16)

    flat_g = lax.optimization_barrier(flat_g)

    first_mask = n_s // 2
    branches = [
        functools.partial(exchange, mask, sizes) for mask in range(first_mask, 2 * first_mask)
    ]
    evicted, grad_in, held, g_all, keys = lax.switch(
        partner[0] - first_mask, branches, inputs, stash[0, 0], input_grad, partial, flat_g
    )

    evicted, grad_in, key_out, weight_grad = finish(
        head_count, head_size, evicted, grad_in, held, g_all, keys, fwd_positions[0]
    )
    return key_out[None, None], grad_in[None, None], evicted[None, None], weight_grad[None]


def solution(mesh):
    sizes = (mesh.shape["section"], mesh.shape["tensor"], mesh.shape["dp"])
    placed = (
        P("dp", "section", None, "tensor"),
        P("dp", "section", None),
        P("section", "tensor", None, None),
        P("dp", "section", None, "tensor"),
        P(),
        P("dp", "section", None, None, None),
        P("dp", "section", None),
    )
    return jax.shard_map(
        functools.partial(body, sizes),
        mesh=mesh,
        in_specs=placed,
        out_specs=(
            P("dp", "section", "tensor", None, None),
            P("dp", "section", None, "tensor"),
            P("dp", "section", None, "tensor"),
            P("section", ("tensor", "dp"), None, None),
        ),
        check_vma=False,
    )
```

time: 79.4 us -> 73.2 us (0.922)
  the two profiles are of different devices: /device:TPU:38 before, /device:TPU:81 now
where the time goes in v2:
time: 73.2 us; the launch traced here: 72.5 us
  Pallas kernels  66.2 us (90%)
  matrix products  2.13 us (3%)
  local copies, waits for them, and re-layouts  1.95 us (3%)
  other arithmetic  1.41 us (2%)
  between operations  0.78 us (1%)
    pallas_call x1, Pallas kernels, exchange(): pl.pallas_call(functools.partial(exchange_kernel, mask, sizes), out_shape...  64.1 us
    pallas_call x1, Pallas kernels, finish(): pl.pallas_call(finish_kernel, out_shape=[jax.ShapeDtypeStruct(shape, dtyp...  2.09 us
    unnamed x13, local copies, waits for them, and re-layouts  1.95 us
    dot_general x1, matrix products, body(): jnp.dot(inputs, flat_weight, preferred_element_type=jnp.float32)  1.65 us

profile of v2, /device:TPU:81, one launch (start us, length us, event | category | flops | bytes accessed | tf_op | source)
XLA Modules:
  0.0 72.5 jit_solution(3954682298695853245)
XLA Ops:
  0.6 0.0 copy-start.4
  0.6 0.6 copy-done.4
  1.3 0.0 copy-start.5
  1.4 0.6 maximum_bitcast_fusion.freqs
  1.9 0.1 copy-done.5
  2.0 0.3 multiply_cosine_fusion
  2.3 0.0 copy-start.2
  2.3 1.7 %convolution_convert_fusion.1 = bf16[128,512]{1,0:T(8,128)(2,1)S(1)} fusion(bf16[128,8,4,128]{3,2,1,0:T(4,128)(2,1)} %bitcast.113, bf16[1,1,128,1024]{3,2,1,0:T(8,128)(2,1)} %param.23), kind=kOutput, calls=%fused_computation.1 | convolution fusion | flops 134283264 | bytes 1441792 | tf_op jit(solution)/shard_map/dot_general | solution.py:301
  4.0 0.0 copy-done.2
  4.0 0.0 copy-start.3
  4.1 0.3 multiply_subtract_fusion
  4.3 0.2 maximum_convert_fusion
  4.6 0.7 copy-done.3
  5.2 0.0 copy-start
  5.2 0.0 copy-start.1
  5.2 0.5 convolution_convert_fusion
  5.7 0.5 copy-done
  6.2 0.1 copy-done.1
  6.3 64.2 %conditional.1 = ((bf16[128,1024]{1,0:T(8,128)(2,1)S(1)}, bf16[128,1024]{1,0:T(8,128)(2,1)S(1)}, bf16[4,128,256]{2,1,0:T(8,128)(2,1)S(1)}, bf16[4,128,512]{2,1,0:T(8,128)(2,1)S(1)}, bf16[2,16,512]{2,1,0:T(8,128)(2,1)S(1)})) conditional(s32[]{:T(128)} %bitcast.16, (bf16[128,512]{1,0:T(8,128)(2,1)S(1)}, ...), branch_computations={%region_0.0_spmd, %region_1.0_spmd, %region_2.0_spmd, %region_3.0_... | conditional | bytes 8 | solution.py:315
  6.3 64.1 %exchange_25.1 = (bf16[128,1024]{1,0:T(8,128)(2,1)S(1)}, bf16[128,1024]{1,0:T(8,128)(2,1)S(1)}, bf16[4,128,256]{2,1,0:T(8,128)(2,1)S(1)}, bf16[4,128,512]{2,1,0:T(8,128)(2,1)S(1)}, bf16[2,16,512]{2,1,0:T(8,128)(2,1)S(1)}) custom-call(bf16[128,1024]{1,0:T(8,128)(2,1)S(1)} %get-tuple-element.205.fwd, bf16[128,1024]{1,0:T(8,128)(2,1)S(1)} %get-tuple-element.206.stash, ...), custom_call_target="tpu_custom_call" | custom-call | tf_op jit(solution)/shard_map/cond/branch_9_fun/exchange_25/pallas_call | solution.py:208
  70.4 2.1 %finish.1 = (bf16[128,1024]{1,0:T(8,128)(2,1)}, bf16[128,1024]{1,0:T(8,128)(2,1)}, bf16[16,4,128]{2,1,0:T(4,128)(2,1)}, bf16[256,4,128]{2,1,0:T(4,128)(2,1)}) custom-call(bf16[128,1024]{1,0:T(8,128)(2,1)S(1)} %get-tuple-element.253.evicted, bf16[128,1024]{1,0:T(8,128)(2,1)S(1)} %get-tuple-element.254.grad_in, ...), custom_call_target="tpu_custom_call" | custom-call | tf_op jit(solution)/shard_map/finish/pallas_call | solution.py:279
  (4 shorter events, 0.1 us)
Async XLA Ops:
  0.6 0.7 copy-start.4
  1.3 0.7 copy-start.5
  2.3 1.7 %copy-start.2 = (bf16[1,1,128,4,128]{4,3,2,1,0:T(4,128)(2,1)S(1)}, bf16[1,1,128,4,128]{4,3,2,1,0:T(4,128)(2,1)}, u32[]{:S(2)}) copy-start(bf16[1,1,128,4,128]{4,3,2,1,0:T(4,128)(2,1)} %param.28) | copy-start | bytes 393220
  4.0 1.2 %copy-start.3 = (bf16[1,1024,4,128]{3,2,1,0:T(4,128)(2,1)S(1)}, bf16[1,1024,4,128]{3,2,1,0:T(4,128)(2,1)}, u32[]{:S(2)}) copy-start(bf16[1,1024,4,128]{3,2,1,0:T(4,128)(2,1)} %param.25) | copy-start | bytes 3145732
  5.2 0.9 %copy-start = (bf16[1,1,128,1024]{3,2,1,0:T(8,128)(2,1)S(1)}, bf16[1,1,128,1024]{3,2,1,0:T(8,128)(2,1)}, u32[]{:S(2)}) copy-start(bf16[1,1,128,1024]{3,2,1,0:T(8,128)(2,1)} %param.23) | copy-start | bytes 786436
  5.2 1.0 %copy-start.1 = (bf16[1,1,128,1024]{3,2,1,0:T(8,128)(2,1)S(1)}, bf16[1,1,128,1024]{3,2,1,0:T(8,128)(2,1)}, u32[]{:S(2)}) copy-start(bf16[1,1,128,1024]{3,2,1,0:T(8,128)(2,1)} %param.26) | copy-start | bytes 786436
